TPU v7x, 512 devices: a whole 4x4x16 slice. The times are simulated.
512 devices in a mesh: dp: 16 (over z), pipe: 4 (over x), tensor: 8 (over y, core).
Axes of the slice: x: 4, y: 4, z: 16, core: 2. Of those that a mesh axis runs over, the one named last changes fastest.
Arguments:
- tokens: bfloat16 [16384, 8192], P('dp', ('pipe', 'tensor')), may hold values from -6 to 6
- key_value_weight: bfloat16 [8192, 2048], P(('pipe', 'tensor')), may hold values from -0.0625 to 0.0625
- adapter_down: bfloat16 [96, 8192, 128], P(None, ('pipe', 'tensor', 'dp')), may hold values from -0.0625 to 0.0625
- adapter_up: bfloat16 [96, 64, 2048], P(None, 'dp'), may hold values from -0.75 to 0.75
- tenant_of_block: int32 [128], replicated, may hold values from 0 to 95
- slot_of_tenant: int32 [96], replicated, may hold values from 0 to 95, each once
- cotangent: bfloat16 [16384, 2048], P(('dp', 'pipe', 'tensor')), may hold values from -1.5 to 1.5
Outputs:
- key_value: bfloat16 [16384, 2048], P(('dp', 'pipe', 'tensor'))
- input_grad: bfloat16 [16384, 8192], P('dp', ('pipe', 'tensor'))
- grad_a: float32 [96, 8192, 128], P(None, ('pipe', 'tensor', 'dp'))
- grad_b: float32 [96, 64, 2048], P(None, 'dp', ('pipe', 'tensor'))
Inputs may be any that keep to these rules, and one draw needn't show every extreme that they name: `slot_of_tenant`: each slot holds exactly one tenant.
All inputs are finite; a program needn't handle non-finite values.
Results may differ from a plain program's by a relative error of at most 0.017.
Values may be sent and summed in bfloat16 or wider, within the bound.
A program may use at most 64 MiB of HBM per device.

v0:
```python
import jax
import jax.numpy as jnp
from jax import lax
from jax.sharding import PartitionSpec as P

KEY_WIDTH = 1024
ADAPTER_RANK = 64
BLOCK = 128


def body(
    tokens, key_value_weight, adapter_down, adapter_up, tenant_of_block, slot_of_tenant, cotangent
):
    data_count = lax.axis_size("dp")
    group_count = lax.axis_size(("pipe", "tensor"))
    my_group = lax.axis_index(("pipe", "tensor"))
    tok_dev, feature_count = tokens.shape
    blocks_dev = tok_dev // BLOCK
    row_count = tok_dev // group_count
    tenant_list = slot_of_tenant.shape[0]
    all_blocks = tenant_of_block.shape[0]
    tenant_ids = lax.broadcasted_iota(jnp.int32, (all_blocks, tenant_list), 1)
    slot_of_block = jnp.sum(
        jnp.where(tenant_of_block[:, None] == tenant_ids, slot_of_tenant[None, :], 0), axis=1
    )
    slot_match = slot_of_block[:, None] == tenant_ids
    down_rows = adapter_down.shape[1]
    a_send = jnp.dot(
        slot_match.astype(jnp.bfloat16),
        adapter_down.reshape(tenant_list, down_rows * 2 * ADAPTER_RANK),
        preferred_element_type=jnp.float32,
    )
    a_send = a_send.astype(jnp.bfloat16).reshape(all_blocks, down_rows, 2 * ADAPTER_RANK)
    own_block = my_group * row_count // BLOCK
    own_slots = lax.dynamic_index_in_dim(
        slot_of_block.reshape(data_count, blocks_dev), own_block, 1, False
    )
    owner_choice = (
        own_slots[:, None] == lax.broadcasted_iota(jnp.int32, (data_count, tenant_list), 1)
    ).astype(jnp.bfloat16)
    up_rows = adapter_up.shape[1]
    b_send = jnp.dot(
        owner_choice,
        adapter_up.reshape(tenant_list, up_rows * 2 * KEY_WIDTH),
        preferred_element_type=jnp.float32,
    )
    b_send = b_send.astype(jnp.bfloat16).reshape(data_count, up_rows, 2 * KEY_WIDTH)
    down_blocks, b_own = (
        lax.all_to_all(a_send, "dp", split_axis=0, concat_axis=1, tiled=True),
        lax.all_to_all(b_send, "dp", split_axis=0, concat_axis=1, tiled=True),
    )
    b_own = b_own[0]
    tok_blocks = tokens.reshape(blocks_dev, BLOCK, feature_count)
    low_part = jnp.einsum(
        "bif,bfr->bir", tok_blocks, down_blocks, preferred_element_type=jnp.float32
    ).reshape(tok_dev, 2 * ADAPTER_RANK)
    low_all = lax.psum(low_part.astype(jnp.bfloat16), ("pipe", "tensor"))
    base_out = lax.psum_scatter(
        jnp.dot(tokens, key_value_weight, preferred_element_type=jnp.float32).astype(jnp.bfloat16),
        ("pipe", "tensor"),
        scatter_dimension=0,
        tiled=True,
    ).astype(jnp.float32)
    low_rows = lax.dynamic_slice_in_dim(low_all, my_group * row_count, row_count, 0)
    lowrank = jnp.concatenate(
        [
            jnp.dot(
                low_rows[:, :ADAPTER_RANK], b_own[:, :KEY_WIDTH], preferred_element_type=jnp.float32
            ),
            jnp.dot(
                low_rows[:, ADAPTER_RANK:], b_own[:, KEY_WIDTH:], preferred_element_type=jnp.float32
            ),
        ],
        axis=1,
    )
    key_value = (base_out + lowrank).astype(jnp.bfloat16)
    contract_last = (((1,), (1,)), ((), ()))
    grad_rows = jnp.concatenate(
        [
            lax.dot_general(
                cotangent[:, :KEY_WIDTH],
                b_own[:, :KEY_WIDTH],
                contract_last,
                preferred_element_type=jnp.float32,
            ),
            lax.dot_general(
                cotangent[:, KEY_WIDTH:],
                b_own[:, KEY_WIDTH:],
                contract_last,
                preferred_element_type=jnp.float32,
            ),
        ],
        axis=1,
    )
    grad_rows = grad_rows.astype(jnp.bfloat16)
    cot_all, grad_low = (
        lax.all_gather(cotangent, ("pipe", "tensor"), axis=0, tiled=True),
        lax.all_gather(grad_rows, ("pipe", "tensor"), axis=0, tiled=True),
    )
    grad_blocks = grad_low.reshape(blocks_dev, BLOCK, 2 * ADAPTER_RANK)
    input_grad = lax.dot_general(
        cot_all, key_value_weight, contract_last, preferred_element_type=jnp.float32
    )
    input_grad = input_grad + jnp.einsum(
        "bir,bfr->bif", grad_blocks, down_blocks, preferred_element_type=jnp.float32
    ).reshape(tok_dev, feature_count)
    input_grad = input_grad.astype(jnp.bfloat16)
    grad_a_part = jnp.einsum(
        "bif,bir->bfr", tok_blocks, grad_blocks, preferred_element_type=jnp.float32
    )
    col_count = 2 * KEY_WIDTH // group_count
    col_start = my_group * col_count
    half_index = col_start // KEY_WIDTH
    low_half = lax.dynamic_slice_in_dim(
        low_all, half_index * ADAPTER_RANK, ADAPTER_RANK, 1
    ).reshape(blocks_dev, BLOCK, ADAPTER_RANK)
    cot_cols = lax.dynamic_slice_in_dim(cot_all, col_start, col_count, 1).reshape(
        blocks_dev, BLOCK, col_count
    )
    grad_b_part = jnp.einsum("bir,bic->brc", low_half, cot_cols, preferred_element_type=jnp.float32)
    grad_a_recv, grad_b_recv = (
        lax.all_to_all(
            grad_a_part.astype(jnp.bfloat16), "dp", split_axis=1, concat_axis=0, tiled=True
        ).astype(grad_a_part.dtype),
        lax.all_to_all(
            grad_b_part.astype(jnp.bfloat16), "dp", split_axis=1, concat_axis=0, tiled=True
        ).astype(grad_b_part.dtype),
    )
    slot_weight = slot_match.astype(jnp.float32)
    grad_a = jnp.einsum(
        "bt,bx->tx",
        slot_weight,
        grad_a_recv.reshape(all_blocks, down_rows * 2 * ADAPTER_RANK),
        precision=lax.Precision.HIGHEST,
    )
    grad_a = grad_a.reshape(tenant_list, down_rows, 2 * ADAPTER_RANK)
    grad_b = jnp.einsum(
        "bt,bx->tx",
        slot_weight,
        grad_b_recv.reshape(all_blocks, grad_b_recv.shape[1] * col_count),
        precision=lax.Precision.HIGHEST,
    )
    grad_b = grad_b.reshape(tenant_list, grad_b_recv.shape[1], col_count)
    return (key_value, input_grad, grad_a, grad_b)


def solution(mesh):
    placed = (
        P("dp", ("pipe", "tensor")),
        P(("pipe", "tensor"), None),
        P(None, ("pipe", "tensor", "dp"), None),
        P(None, "dp", None),
        P(),
        P(),
        P(("dp", "pipe", "tensor"), None),
    )
    return jax.shard_map(
        body,
        mesh=mesh,
        in_specs=placed,
        out_specs=(
            P(("dp", "pipe", "tensor"), None),
            P("dp", ("pipe", "tensor")),
            P(None, ("pipe", "tensor", "dp"), None),
            P(None, "dp", ("pipe", "tensor")),
        ),
        check_vma=False,
    )
```

profile of v0, /device:TPU:2, one launch (start us, length us, event | category | flops | bytes accessed | tf_op | source)
XLA Modules:
  0.0 395.1 jit_solution(17106891758424243477)
XLA Ops:
  7.2 0.9 select_reduce_fusion
  8.1 1.3 fusion.2
  9.5 0.1 copy.60
  9.6 44.1 %all_to_all.57 = bf16[128,16,128]{2,1,0:T(8,128)(2,1)S(1)} all-to-all(bf16[128,16,128]{2,1,0:T(8,128)(2,1)S(1)} %bitcast.78), channel_id=1, replica_groups=mesh['dp'=16,'pipe'=4,'tensor'=8] {'dp'}, dimensions={0} | all-to-all | bytes 1048576 | tf_op jit(solution)/shard_map/all_to_all | solution.py:49
  53.7 0.8 copy-done.2
  54.5 0.3 convolution_convert_fusion.4
  54.8 0.9 copy.41
  55.7 0.0 reduce-scatter.2.cloned.1.call-start
  55.7 3.2 convolution_convert_fusion.1
  59.0 0.0 all-gather.2.cloned.1.call-start
  59.1 0.7 all-gather.2.cloned.1.call-update
  59.8 0.1 reshape.62
  59.8 2.4 copy.61
  62.3 0.2 dynamic-slice_reduce_fusion
  62.5 0.4 convolution_convert_fusion
  62.9 0.2 reshape.64
  63.0 24.5 %all_to_all.58 = bf16[16,4,2048]{2,1,0:T(4,128)(2,1)S(1)} all-to-all(bf16[16,4,2048]{2,1,0:T(4,128)(2,1)S(1)} %reshape.64), channel_id=1, replica_groups=mesh['dp'=16,'pipe'=4,'tensor'=8] {'dp'}, dimensions={0} | all-to-all | bytes 524288 | tf_op jit(solution)/shard_map/all_to_all | solution.py:50
  87.5 0.1 squeeze.5
  87.6 0.1 fusion.3
  87.8 0.2 fusion.4
  87.9 0.4 copy-done.4
  88.3 0.1 pad_maximum_fusion
  88.4 24.9 %all_gather.7 = bf16[1024,128]{1,0:T(8,128)(2,1)S(1)} all-gather(bf16[32,128]{1,0:T(8,128)(2,1)S(1)} %pad_maximum_fusion), channel_id=1, replica_groups=mesh['dp'=16,'pipe'=4,'tensor'=8] {'pipe','tensor'}, dimensions={0}, use_global_device_ids=true | all-gather | bytes 270336 | tf_op jit(solution)/shard_map/all_gather | solution.py:98
  113.3 0.3 fusion.1
  113.6 1.1 copy.43
  114.7 5.8 %all-to-all-start.2 = ((bf16[8,256,128]{2,0,1:T(8,128)(2,1)}), bf16[8,256,128]{2,0,1:T(8,128)(2,1)S(1)}, u32[]{:S(2)}, u32[]{:S(2)}) async-start(bf16[8,256,128]{2,0,1:T(8,128)(2,1)} %copy.43), calls=%async_computation.3 | async-start | bytes 1048576 | tf_op jit(solution)/shard_map/all_to_all | solution.py:122
  120.5 0.3 fusion.30
  120.8 63.9 %all-reduce.2.cloned.1.call-done = bf16[1024,128]{0,1:T(8,128)(2,1)} async-done(((bf16[1024,128]{0,1:T(8,128)(2,1)}), bf16[1024,128]{0,1:T(8,128)(2,1)}) %all-reduce.2.cloned.1.call-update) | async-done | bytes 262160 | tf_op jit(solution)/shard_map/psum | solution.py:57
  184.8 1.2 fusion.14
  185.9 1.2 fusion.11
  187.1 0.3 copy.46
  187.4 0.3 fusion.21
  187.7 1.3 copy.53
  189.1 105.7 %reduce-scatter.2.cloned.1.call-done = bf16[32,2048]{1,0:T(8,128)(2,1)} async-done(((bf16[1024,2048]{1,0:T(8,128)(2,1)}), bf16[32,2048]{1,0:T(8,128)(2,1)}) %reduce-scatter.2.cloned.1.call-update) | async-done | bytes 131088 | tf_op jit(solution)/shard_map/reduce_scatter | solution.py:58
  294.8 1.6 fusion.7
  296.4 62.4 %all-gather.2.cloned.1.call-done = bf16[1024,2048]{1,0:T(8,128)(2,1)} async-done(((bf16[32,2048]{1,0:T(8,128)(2,1)}), bf16[1024,2048]{1,0:T(8,128)(2,1)}) %all-gather.2.cloned.1.call-update) | async-done | bytes 4194320 | tf_op jit(solution)/shard_map/all_gather | solution.py:97
  358.8 1.1 constant_dynamic-slice_fusion
  359.9 1.1 convolution_convert_fusion.5
  361.0 0.1 copy.73
  361.1 0.8 reshape.73
  361.9 12.3 %all-to-all-start.3 = ((bf16[16,2,1024]{2,1,0:T(2,128)(2,1)}), bf16[16,2,1024]{2,1,0:T(2,128)(2,1)S(1)}, u32[]{:S(2)}, u32[]{:S(2)}) async-start(bf16[16,2,1024]{2,1,0:T(2,128)(2,1)} %reshape.73), calls=%async_computation.4 | async-start | bytes 131072 | tf_op jit(solution)/shard_map/all_to_all | solution.py:125
  374.2 4.3 %fusion = bf16[1024,256]{1,0:T(8,128)(2,1)} fusion(f32[1024,256]{1,0:T(8,128)S(1)} %bitcast.81, bf16[1024,2048]{1,0:T(8,128)(2,1)} %all-gather.2.cloned.1.call-done, bf16[256,2048]{1,0:T(8,128)(2,1)S(1)} %copy-done), kind=kOutput, calls=%fused_computation.4 | convolution fusion | flops 1074266112 | bytes 6815744 | tf_op jit(solution)/shard_map/dot_general | solution.py:101
  378.4 8.9 %all-to-all-done.3 = bf16[16,2,1024]{2,1,0:T(2,128)(2,1)S(1)} async-done(((bf16[16,2,1024]{2,1,0:T(2,128)(2,1)}), bf16[16,2,1024]{2,1,0:T(2,128)(2,1)S(1)}, u32[]{:S(2)}, u32[]{:S(2)}) %all-to-all-start.3) | async-done | bytes 65568 | tf_op jit(solution)/shard_map/all_to_all | solution.py:125
  387.3 0.1 reshape.74
  387.5 0.1 copy.72
  387.5 0.1 reshape.70
  387.7 0.1 copy.52
  387.8 0.8 fusion.19
  (15 shorter events, 0.1 us)
Async XLA Ops:
  7.2 48.6 %copy-start = (bf16[256,2048]{1,0:T(8,128)(2,1)S(1)}, bf16[256,2048]{1,0:T(8,128)(2,1)}, u32[]{:S(2)}) copy-start(bf16[256,2048]{1,0:T(8,128)(2,1)} %param.8) | copy-start | bytes 3145732
  7.2 47.3 %copy-start.1 = (bf16[1024,256]{1,0:T(8,128)(2,1)S(1)}, bf16[1024,256]{1,0:T(8,128)(2,1)}, u32[]{:S(2)}) copy-start(bf16[1024,256]{1,0:T(8,128)(2,1)} %param.7) | copy-start | bytes 1572868
  7.2 177.6 %all-reduce.2.cloned.1.call-start = ((), (), s32[]{:S(2)}) async-start(), calls=%async_computation.6 | async-start | bytes 524288 | tf_op jit(solution)/shard_map/psum | solution.py:57
  53.7 0.8 copy-start.2
  55.7 239.1 %reduce-scatter.2.cloned.1.call-start = ((), (), s32[]{:S(2)}) async-start(), calls=%async_computation.5 | async-start | bytes 4325376 | tf_op jit(solution)/shard_map/reduce_scatter | solution.py:58
  59.0 28.6 %copy-start.5 = (bf16[32,2048]{1,0:T(8,128)(2,1)S(1)}, bf16[32,2048]{1,0:T(8,128)(2,1)}, u32[]{:S(2)}) copy-start(bf16[32,2048]{1,0:T(8,128)(2,1)} %param.13) | copy-start | bytes 393220
  59.0 299.8 %all-gather.2.cloned.1.call-start = ((), (), s32[]{:S(2)}) async-start(), calls=%async_computation.7 | async-start | bytes 4325376 | tf_op jit(solution)/shard_map/all_gather | solution.py:97
  62.8 57.7 %copy-start.3 = (bf16[16,8,16,128]{3,2,0,1:T(8,128)(2,1)S(1)}, bf16[16,8,16,128]{3,2,0,1:T(8,128)(2,1)}, u32[]{:S(2)}) copy-start(bf16[16,8,16,128]{3,2,0,1:T(8,128)(2,1)} %copy-done.2) | copy-start | bytes 1572868
  87.6 0.7 copy-start.4
  114.7 72.4 %all-to-all-start.2 = ((bf16[8,256,128]{2,0,1:T(8,128)(2,1)}), bf16[8,256,128]{2,0,1:T(8,128)(2,1)S(1)}, u32[]{:S(2)}, u32[]{:S(2)}) async-start(bf16[8,256,128]{2,0,1:T(8,128)(2,1)} %copy.43), calls=%async_computation.3 | async-start | bytes 1048576 | tf_op jit(solution)/shard_map/all_to_all | solution.py:122
  361.9 25.5 %all-to-all-start.3 = ((bf16[16,2,1024]{2,1,0:T(2,128)(2,1)}), bf16[16,2,1024]{2,1,0:T(2,128)(2,1)S(1)}, u32[]{:S(2)}, u32[]{:S(2)}) async-start(bf16[16,2,1024]{2,1,0:T(2,128)(2,1)} %reshape.73), calls=%async_computation.4 | async-start | bytes 131072 | tf_op jit(solution)/shard_map/all_to_all | solution.py:125
Sparse Core Ops, SparseCore 0:
  55.8 128.9 all-reduce.1
  189.3 105.4 reduce-scatter.1
  297.9 60.8 all-gather.1
where the time goes:
time: 396 us; the launch traced here: 395 us
  waiting for transfers between devices  242 us (61%)
  blocking collectives  93.4 us (24%)
  starting transfers between devices  18.2 us (5%)
  matrix products  15 us (4%)
  between operations  14 us (4%)
  local copies, waits for them, and re-layouts  10.2 us (3%)
    reduce_scatter x1, waiting for transfers between devices, body(): lax.psum_scatter(jnp.dot(tokens, key_value_weight, preferred_element_type...  106 us
    psum x1, waiting for transfers between devices, body(): low_all = lax.psum(low_part.astype(jnp.bfloat16), ('pipe', 'tensor'))  63.9 us
    all_gather x1, waiting for transfers between devices, body(): lax.all_gather(cotangent, ('pipe', 'tensor'), axis=0, tiled=True)  62.4 us
    all_to_all x1, blocking collectives, body(): lax.all_to_all(a_send, 'dp', split_axis=0, concat_axis=1, tiled=True)  44.1 us
    all_gather x1, blocking collectives, body(): lax.all_gather(grad_rows, ('pipe', 'tensor'), axis=0, tiled=True)  24.9 us
    all_to_all x1, blocking collectives, body(): lax.all_to_all(b_send, 'dp', split_axis=0, concat_axis=1, tiled=True)  24.5 us
    all_to_all x1, starting transfers between devices, body(): lax.all_to_all(grad_b_part.astype(jnp.bfloat16), 'dp', split_axis=1, conc...  12.3 us
    all_to_all x1, waiting for transfers between devices, body(): lax.all_to_all(grad_b_part.astype(jnp.bfloat16), 'dp', split_axis=1, conc...  8.89 us
  transfers between devices with their start and end apart: 5, of which 4 were waited for; matrix products, arithmetic and copies ran while one was open for 5% of the time, Pallas kernels for 0%

commit v1 on v0

--- a/solution.py
+++ b/solution.py
@@ -54,7 +54,7 @@
     low_part = jnp.einsum(
         "bif,bfr->bir", tok_blocks, down_blocks, preferred_element_type=jnp.float32
     ).reshape(tok_dev, 2 * ADAPTER_RANK)
-    low_all = lax.psum(low_part.astype(jnp.bfloat16), ("pipe", "tensor"))
+    low_all = lax.psum(lax.psum(low_part.astype(jnp.bfloat16), "pipe"), "tensor")
     base_out = lax.psum_scatter(
         jnp.dot(tokens, key_value_weight, preferred_element_type=jnp.float32).astype(jnp.bfloat16),
         ("pipe", "tensor"),

time: 396 us -> 322 us (0.81)
  waiting for transfers between devices: 242 us -> 163 us
  blocking collectives: 93.4 us -> 97.5 us
    reduce_scatter x1, waiting for transfers between devices: 106 us -> 12.4 us  [body(): lax.psum_scatter(jnp.dot(tokens, key_value_weight, preferred_element_type...]
    all_to_all x1, waiting for transfers between devices: 0.01 us -> 11.7 us  [body(): lax.all_to_all(grad_a_part.astype(jnp.bfloat16), 'dp', split_axis=1, conc...]
    all_to_all x1, blocking collectives: 24.5 us -> 29 us  [body(): lax.all_to_all(b_send, 'dp', split_axis=0, concat_axis=1, tiled=True)]
    psum x1 -> x2, waiting for transfers between devices: 63.9 us -> 67 us  [the longest x1 52 us: body(): lax.psum(low_part.astype(jnp.bfloat16), 'pipe')]
  transfers between devices with their start and end apart: 5 -> 6, of which waited for: 4 -> 6; matrix products, arithmetic and copies ran while one was open for 5% -> 6% of each run, Pallas kernels for 0% -> 0%
where the time goes in v1:
time: 322 us
  waiting for transfers between devices  163 us (51%)
  blocking collectives  97.5 us (30%)
  starting transfers between devices  17.7 us (5%)
  between operations  15.8 us (5%)
  matrix products  15 us (5%)
  local copies, waits for them, and re-layouts  10.2 us (3%)
    all_gather x1, waiting for transfers between devices, body(): lax.all_gather(cotangent, ('pipe', 'tensor'), axis=0, tiled=True)  62.3 us
    psum x1, waiting for transfers between devices, body(): lax.psum(low_part.astype(jnp.bfloat16), 'pipe')  52 us
    all_to_all x1, blocking collectives, body(): lax.all_to_all(a_send, 'dp', split_axis=0, concat_axis=1, tiled=True)  44.1 us
    all_to_all x1, blocking collectives, body(): lax.all_to_all(b_send, 'dp', split_axis=0, concat_axis=1, tiled=True)  29 us
    all_gather x1, blocking collectives, body(): lax.all_gather(grad_rows, ('pipe', 'tensor'), axis=0, tiled=True)  24.4 us
    psum x1, waiting for transfers between devices, body(): lax.psum(lax.psum(low_part.astype(jnp.bfloat16), 'pipe'), 'tensor')  15 us
    reduce_scatter x1, waiting for transfers between devices, body(): lax.psum_scatter(jnp.dot(tokens, key_value_weight, preferred_element_type...  12.4 us
    all_to_all x1, starting transfers between devices, body(): lax.all_to_all(grad_b_part.astype(jnp.bfloat16), 'dp', split_axis=1, conc...  12.3 us
  transfers between devices with their start and end apart: 6, of which 6 were waited for; matrix products, arithmetic and copies ran while one was open for 6% of the time, Pallas kernels for 0%

profile of v1, /device:TPU:2, one launch (start us, length us, event | category | flops | bytes accessed | tf_op | source)
XLA Modules:
  0.0 321.5 jit_solution(1179407160290872442)
XLA Ops:
  8.1 0.9 select_reduce_fusion
  9.0 1.3 fusion.2
  10.3 0.1 copy.60
  10.4 44.1 %all_to_all.57 = bf16[128,16,128]{2,1,0:T(8,128)(2,1)S(1)} all-to-all(bf16[128,16,128]{2,1,0:T(8,128)(2,1)S(1)} %bitcast.78), channel_id=1, replica_groups=mesh['dp'=16,'pipe'=4,'tensor'=8] {'dp'}, dimensions={0} | all-to-all | bytes 1048576 | tf_op jit(solution)/shard_map/all_to_all | solution.py:49
  54.5 0.8 copy-done.2
  55.3 0.3 convolution_convert_fusion.4
  55.6 0.9 copy.41
  56.5 52.0 %all-reduce.3.cloned.1.call-done = bf16[1024,128]{0,1:T(8,128)(2,1)} async-done(((bf16[1024,128]{0,1:T(8,128)(2,1)}), bf16[1024,128]{0,1:T(8,128)(2,1)}) %all-reduce.3.cloned.1.call-update) | async-done | bytes 262160 | tf_op jit(solution)/shard_map/psum | solution.py:57
  108.6 3.2 %convolution_convert_fusion.1 = bf16[1024,2048]{1,0:T(8,128)(2,1)} fusion(bf16[1024,256]{1,0:T(8,128)(2,1)S(1)} %copy-done.1, bf16[256,2048]{1,0:T(8,128)(2,1)S(1)} %copy-done), kind=kOutput, calls=%fused_computation.1 | convolution fusion | flops 1075838976 | bytes 5767168 | tf_op jit(solution)/shard_map/dot_general | solution.py:59
  111.9 0.5 all-gather.2.cloned.1.call-update
  112.5 0.1 reshape.62
  112.6 2.4 copy.61
  115.0 0.2 dynamic-slice_reduce_fusion
  115.2 0.4 convolution_convert_fusion
  115.6 0.2 reshape.64
  115.8 29.0 %all_to_all.58 = bf16[16,4,2048]{2,1,0:T(4,128)(2,1)S(1)} all-to-all(bf16[16,4,2048]{2,1,0:T(4,128)(2,1)S(1)} %reshape.64), channel_id=1, replica_groups=mesh['dp'=16,'pipe'=4,'tensor'=8] {'dp'}, dimensions={0} | all-to-all | bytes 524288 | tf_op jit(solution)/shard_map/all_to_all | solution.py:50
  144.8 0.1 squeeze.5
  144.9 0.1 fusion.3
  145.0 0.2 fusion.4
  145.2 0.4 copy-done.4
  145.6 0.1 pad_maximum_fusion
  145.7 24.4 %all_gather.7 = bf16[1024,128]{1,0:T(8,128)(2,1)S(1)} all-gather(bf16[32,128]{1,0:T(8,128)(2,1)S(1)} %pad_maximum_fusion), channel_id=1, replica_groups=mesh['dp'=16,'pipe'=4,'tensor'=8] {'pipe','tensor'}, dimensions={0}, use_global_device_ids=true | all-gather | bytes 270336 | tf_op jit(solution)/shard_map/all_gather | solution.py:98
  170.1 0.3 fusion.1
  170.4 1.1 copy.43
  171.5 5.2 %all-to-all-start.2 = ((bf16[8,256,128]{2,0,1:T(8,128)(2,1)}), bf16[8,256,128]{2,0,1:T(8,128)(2,1)S(1)}, u32[]{:S(2)}, u32[]{:S(2)}) async-start(bf16[8,256,128]{2,0,1:T(8,128)(2,1)} %copy.43), calls=%async_computation.3 | async-start | bytes 1048576 | tf_op jit(solution)/shard_map/all_to_all | solution.py:122
  176.8 0.3 fusion.30
  177.1 15.0 %all-reduce.5.cloned.1.call-done = bf16[1024,128]{0,1:T(8,128)(2,1)} async-done(((bf16[1024,128]{0,1:T(8,128)(2,1)}), bf16[1024,128]{0,1:T(8,128)(2,1)}) %all-reduce.5.cloned.1.call-update) | async-done | bytes 262160 | tf_op jit(solution)/shard_map/psum | solution.py:57
  192.1 1.2 fusion.14
  193.2 1.2 fusion.11
  194.4 11.7 %all-to-all-done.2 = bf16[8,256,128]{2,0,1:T(8,128)(2,1)S(1)} async-done(((bf16[8,256,128]{2,0,1:T(8,128)(2,1)}), bf16[8,256,128]{2,0,1:T(8,128)(2,1)S(1)}, u32[]{:S(2)}, u32[]{:S(2)}) %all-to-all-start.2) | async-done | bytes 524320 | tf_op jit(solution)/shard_map/all_to_all | solution.py:122
  206.1 0.3 copy.46
  206.4 0.3 fusion.21
  206.7 1.3 copy.53
  208.0 12.4 %reduce-scatter.2.cloned.1.call-done = bf16[32,2048]{1,0:T(8,128)(2,1)} async-done(((bf16[1024,2048]{1,0:T(8,128)(2,1)}), bf16[32,2048]{1,0:T(8,128)(2,1)}) %reduce-scatter.2.cloned.1.call-update) | async-done | bytes 131088 | tf_op jit(solution)/shard_map/reduce_scatter | solution.py:58
  220.4 1.6 fusion.7
  222.0 62.3 %all-gather.2.cloned.1.call-done = bf16[1024,2048]{1,0:T(8,128)(2,1)} async-done(((bf16[32,2048]{1,0:T(8,128)(2,1)}), bf16[1024,2048]{1,0:T(8,128)(2,1)}) %all-gather.2.cloned.1.call-update) | async-done | bytes 4194320 | tf_op jit(solution)/shard_map/all_gather | solution.py:97
  284.2 1.1 constant_dynamic-slice_fusion
  285.3 1.1 convolution_convert_fusion.5
  286.5 0.1 copy.73
  286.6 0.8 reshape.73
  287.3 12.3 %all-to-all-start.3 = ((bf16[16,2,1024]{2,1,0:T(2,128)(2,1)}), bf16[16,2,1024]{2,1,0:T(2,128)(2,1)S(1)}, u32[]{:S(2)}, u32[]{:S(2)}) async-start(bf16[16,2,1024]{2,1,0:T(2,128)(2,1)} %reshape.73), calls=%async_computation.4 | async-start | bytes 131072 | tf_op jit(solution)/shard_map/all_to_all | solution.py:125
  299.6 4.3 %fusion = bf16[1024,256]{1,0:T(8,128)(2,1)} fusion(f32[1024,256]{1,0:T(8,128)S(1)} %bitcast.81, bf16[1024,2048]{1,0:T(8,128)(2,1)} %all-gather.2.cloned.1.call-done, bf16[256,2048]{1,0:T(8,128)(2,1)S(1)} %copy-done), kind=kOutput, calls=%fused_computation.4 | convolution fusion | flops 1074266112 | bytes 6815744 | tf_op jit(solution)/shard_map/dot_general | solution.py:101
  303.9 8.9 %all-to-all-done.3 = bf16[16,2,1024]{2,1,0:T(2,128)(2,1)S(1)} async-done(((bf16[16,2,1024]{2,1,0:T(2,128)(2,1)}), bf16[16,2,1024]{2,1,0:T(2,128)(2,1)S(1)}, u32[]{:S(2)}, u32[]{:S(2)}) %all-to-all-start.3) | async-done | bytes 65568 | tf_op jit(solution)/shard_map/all_to_all | solution.py:125
  312.8 0.1 reshape.74
  312.9 0.1 copy.72
  313.0 0.1 reshape.70
  313.1 0.1 copy.52
  313.2 0.8 fusion.19
  (18 shorter events, 0.3 us)
Async XLA Ops:
  8.0 100.6 %copy-start = (bf16[256,2048]{1,0:T(8,128)(2,1)S(1)}, bf16[256,2048]{1,0:T(8,128)(2,1)}, u32[]{:S(2)}) copy-start(bf16[256,2048]{1,0:T(8,128)(2,1)} %param.8) | copy-start | bytes 3145732
  8.0 47.3 %copy-start.1 = (bf16[1024,256]{1,0:T(8,128)(2,1)S(1)}, bf16[1024,256]{1,0:T(8,128)(2,1)}, u32[]{:S(2)}) copy-start(bf16[1024,256]{1,0:T(8,128)(2,1)} %param.7) | copy-start | bytes 1572868
  8.0 100.5 %all-reduce.3.cloned.1.call-start = ((), (), s32[]{:S(2)}) async-start(), calls=%async_computation.6 | async-start | bytes 524288 | tf_op jit(solution)/shard_map/psum | solution.py:57
  54.5 0.8 copy-start.2
  56.5 135.6 %all-reduce.5.cloned.1.call-start = ((), (), s32[]{:S(2)}) async-start(), calls=%async_computation.7 | async-start | bytes 524288 | tf_op jit(solution)/shard_map/psum | solution.py:57
  108.5 111.9 %reduce-scatter.2.cloned.1.call-start = ((), (), s32[]{:S(2)}) async-start(), calls=%async_computation.5 | async-start | bytes 4325376 | tf_op jit(solution)/shard_map/reduce_scatter | solution.py:58
  111.9 33.0 %copy-start.5 = (bf16[32,2048]{1,0:T(8,128)(2,1)S(1)}, bf16[32,2048]{1,0:T(8,128)(2,1)}, u32[]{:S(2)}) copy-start(bf16[32,2048]{1,0:T(8,128)(2,1)} %param.13) | copy-start | bytes 393220
  111.9 172.4 %all-gather.2.cloned.1.call-start = ((), (), s32[]{:S(2)}) async-start(), calls=%async_computation.8 | async-start | bytes 4325376 | tf_op jit(solution)/shard_map/all_gather | solution.py:97
  115.6 61.2 %copy-start.3 = (bf16[16,8,16,128]{3,2,0,1:T(8,128)(2,1)S(1)}, bf16[16,8,16,128]{3,2,0,1:T(8,128)(2,1)}, u32[]{:S(2)}) copy-start(bf16[16,8,16,128]{3,2,0,1:T(8,128)(2,1)} %copy-done.2) | copy-start | bytes 1572868
  144.9 0.7 copy-start.4
  171.5 34.6 %all-to-all-start.2 = ((bf16[8,256,128]{2,0,1:T(8,128)(2,1)}), bf16[8,256,128]{2,0,1:T(8,128)(2,1)S(1)}, u32[]{:S(2)}, u32[]{:S(2)}) async-start(bf16[8,256,128]{2,0,1:T(8,128)(2,1)} %copy.43), calls=%async_computation.3 | async-start | bytes 1048576 | tf_op jit(solution)/shard_map/all_to_all | solution.py:122
  287.3 25.5 %all-to-all-start.3 = ((bf16[16,2,1024]{2,1,0:T(2,128)(2,1)}), bf16[16,2,1024]{2,1,0:T(2,128)(2,1)S(1)}, u32[]{:S(2)}, u32[]{:S(2)}) async-start(bf16[16,2,1024]{2,1,0:T(2,128)(2,1)} %reshape.73), calls=%async_computation.4 | async-start | bytes 131072 | tf_op jit(solution)/shard_map/all_to_all | solution.py:125
Sparse Core Ops, SparseCore 0:
  56.6 51.8 all-reduce.2
  110.8 81.1 all-reduce.4
Sparse Core Ops, SparseCore 1:
  113.5 106.8 reduce-scatter.1
  223.4 60.8 all-gather.1
